TPU v7x, 32 devices: a whole 2x2x4 slice. The times are simulated.
32 devices in a mesh: seq: 8 (over y, x, core), fsdp: 4 (over z).
Axes of the slice: x: 2, y: 2, z: 4, core: 2. Of those that a mesh axis runs over, the one named last changes fastest.
Arguments:
- block_input: bfloat16 [4, 2048, 768], P('fsdp', 'seq'), may hold values from -24 to 24
- out_grad: bfloat16 [4, 2048, 768], P('fsdp', 'seq'), may hold values from -6 to 6
- params: float32 [3768320], P(('seq', 'fsdp')), may hold values from -8 to 8
- first_moment: float32 [3768320], P(('seq', 'fsdp')), may hold values from -3 to 3
- second_moment: float32 [3768320], P(('seq', 'fsdp')), may hold values from 0.01 to 1
Outputs:
- block_output: float32 [4, 2048, 768], P('fsdp', 'seq')
- input_grad: float32 [4, 2048, 768], P('fsdp', 'seq')
- param_grad: float32 [3768320], P(('seq', 'fsdp'))
- new_params: float32 [3768320], P(('seq', 'fsdp'))
- new_first: float32 [3768320], P(('seq', 'fsdp'))
- new_second: float32 [3768320], P(('seq', 'fsdp'))
All inputs are finite; a program needn't handle non-finite values.
Results may differ from a plain program's by a relative error of at most 0.023.
Values may be sent and summed in bfloat16 or wider, within the bound.
A program may use at most 192 MiB of HBM per device.

v0:
```python
import itertools

import jax
import jax.numpy as jnp
from jax import lax
from jax.experimental import pallas as pl
from jax.experimental.layout import Layout, with_layout_constraint
from jax.experimental.pallas import tpu as pltpu
from jax.sharding import PartitionSpec as P

MODEL_WIDTH = 768
MIXER_HEADS = 24
HEAD_DIM = 64
STATE = 128
KERNEL = 4
BLOCK = 256
INNER = 1536
CHANNELS = 1792
PROJ = 3352
RAW = 3765320
PARAMS = 3768320


norm_epsilon = 1e-05
beta_one = 0.9
beta_two = 0.999
learn_rate = 0.02
weight_decay = 0.01
adam_epsilon = 1e-08
adam_step = 2
highest = lax.Precision.HIGHEST


def passed_along(value, axis, by):
    length = lax.axis_size(axis)
    pairs = [(i, i + by) for i in range(length) if 0 <= i + by < length]
    return lax.ppermute(value, axis, pairs)

def silu_grad(pre_act):
    logistic = jax.nn.sigmoid(pre_act)
    return logistic * (1.0 + pre_act * (1.0 - logistic))


def adam_update(weights, gradient, first, second):
    first_new = beta_one * first + (1.0 - beta_one) * gradient
    second_new = beta_two * second + (1.0 - beta_two) * gradient * gradient
    corrected = first_new / (1.0 - beta_one**adam_step)
    scaled = jnp.sqrt(second_new / (1.0 - beta_two**adam_step))
    weights_new = weights - learn_rate * (
        corrected / (scaled + adam_epsilon) + weight_decay * weights
    )
    return (weights_new, first_new, second_new)


LANES = 128
PAIR = 2 * HEAD_DIM
f32 = jnp.float32
bf16 = jnp.bfloat16


def dot_ab(a, b):
    return lax.dot_general(a, b, (((1,), (0,)), ((), ())), preferred_element_type=f32)


def dot_abt(a, b):
    return lax.dot_general(a, b, (((1,), (1,)), ((), ())), preferred_element_type=f32)


def dot_atb(a, b):
    return lax.dot_general(a, b, (((0,), (0,)), ((), ())), preferred_element_type=f32)


def column_of(array, index):
    lane = lax.broadcasted_iota(jnp.int32, array.shape, 1)
    return jnp.sum(jnp.where(lane == index, array, 0.0), axis=1, keepdims=True)


def masked_scores(b_ref, c_ref):
    scores = dot_abt(c_ref[...], b_ref[...])
    row = lax.broadcasted_iota(jnp.int32, scores.shape, 0)
    col = lax.broadcasted_iota(jnp.int32, scores.shape, 1)
    return jnp.where(row >= col, scores, 0.0), row >= col


def inside_kernel(x_ref, b_ref, c_ref, cum_ref, cum_t_ref, dt_t_ref, y_ref, score_ref):
    score_ref[...], _ = masked_scores(b_ref, c_ref)

    def one(pair, carry):
        lanes = pl.ds(pl.multiple_of(pair * PAIR, PAIR), PAIR)
        block = x_ref[:, lanes]
        halves = []
        for side in range(2):
            head = 2 * pair + side
            spread = column_of(cum_ref[...], head) - cum_t_ref[pl.ds(head, 1), :]
            decay = jnp.exp(jnp.minimum(spread, 0.0))
            weights = score_ref[...] * decay * dt_t_ref[pl.ds(head, 1), :]
            halves.append(dot_ab(weights.astype(bf16), block))
        lane = lax.broadcasted_iota(jnp.int32, halves[0].shape, 1)
        y_ref[:, lanes] = jnp.where(lane < HEAD_DIM, halves[0], halves[1])
        return carry

    lax.fori_loop(0, MIXER_HEADS // 2, one, 0)


def inside_grad_kernel(
    x_ref, dy_ref, b_ref, c_ref, cum_ref, cum_t_ref, dt_t_ref,
    dx_ref, db_ref, dc_ref, rows_ref, cols_ref, score_ref, dscore_ref,
):
    score_ref[...], causal = masked_scores(b_ref, c_ref)
    dscore_ref[...] = jnp.zeros_like(dscore_ref)
    rows_ref[...] = jnp.zeros_like(rows_ref)
    row_lane = lax.broadcasted_iota(jnp.int32, rows_ref.shape, 1)

    def one(pair, carry):
        lanes = pl.ds(pl.multiple_of(pair * PAIR, PAIR), PAIR)
        block = x_ref[:, lanes]
        dy = dy_ref[:, lanes]
        lane = lax.broadcasted_iota(jnp.int32, dy.shape, 1)
        halves = []
        for side in range(2):
            head = 2 * pair + side
            mine = (lane < HEAD_DIM) if side == 0 else (lane >= HEAD_DIM)
            dy_head = jnp.where(mine, dy, jnp.zeros_like(dy))
            dt_row = dt_t_ref[pl.ds(head, 1), :]
            spread = column_of(cum_ref[...], head) - cum_t_ref[pl.ds(head, 1), :]
            decay = jnp.exp(jnp.minimum(spread, 0.0))
            scaled = score_ref[...] * decay
            d_weights = dot_abt(dy_head, block)
            halves.append(dot_atb((scaled * dt_row).astype(bf16), dy_head))
            dscore_ref[...] += d_weights * decay * dt_row
            mass = d_weights * scaled
            cols_ref[pl.ds(head, 1), :] = jnp.sum(mass, axis=0, keepdims=True)
            row_sum = jnp.sum(mass * dt_row, axis=1, keepdims=True)
            rows_ref[...] += jnp.where(row_lane == head, row_sum, 0.0)
        dx_ref[:, lanes] = halves[0] + halves[1]
        return carry

    lax.fori_loop(0, MIXER_HEADS // 2, one, 0)
    d_scores = jnp.where(causal, dscore_ref[...], 0.0).astype(bf16)
    dc_ref[...] = dot_ab(d_scores, b_ref[...])
    db_ref[...] = dot_atb(d_scores, c_ref[...])


def whole_vmem(count):
    return [pl.BlockSpec(memory_space=pltpu.VMEM)] * count


def inside_forward(x, b, c, cum, cum_t, dt_t):
    tokens = x.shape[0]
    return pl.pallas_call(
        inside_kernel,
        out_shape=jax.ShapeDtypeStruct((tokens, INNER), f32),
        in_specs=whole_vmem(6),
        out_specs=pl.BlockSpec(memory_space=pltpu.VMEM),
        scratch_shapes=[pltpu.VMEM((tokens, tokens), f32)],
        cost_estimate=pl.CostEstimate(
            flops=4 * tokens * tokens * INNER, bytes_accessed=4 * tokens * INNER,
            transcendentals=tokens * tokens * MIXER_HEADS,
        ),
        name="inside_forward",
    )(x, b, c, cum, cum_t, dt_t)


def inside_backward(x, dy, b, c, cum, cum_t, dt_t):
    tokens = x.shape[0]
    return pl.pallas_call(
        inside_grad_kernel,
        out_shape=(
            jax.ShapeDtypeStruct((tokens, INNER), f32),
            jax.ShapeDtypeStruct((tokens, STATE), f32),
            jax.ShapeDtypeStruct((tokens, STATE), f32),
            jax.ShapeDtypeStruct((tokens, LANES), f32),
            jax.ShapeDtypeStruct((MIXER_HEADS, tokens), f32),
        ),
        in_specs=whole_vmem(7),
        out_specs=tuple(whole_vmem(5)),
        scratch_shapes=[pltpu.VMEM((tokens, tokens), f32), pltpu.VMEM((tokens, tokens), f32)],
        cost_estimate=pl.CostEstimate(
            flops=8 * tokens * tokens * INNER, bytes_accessed=8 * tokens * INNER,
            transcendentals=tokens * tokens * MIXER_HEADS,
        ),
        name="inside_backward",
    )(x, dy, b, c, cum, cum_t, dt_t)


def row_major(array):
    return with_layout_constraint(array, Layout(major_to_minor=(0, 1)))


def head_map():
    owner = lax.broadcasted_iota(jnp.int32, (MIXER_HEADS, INNER), 1) // HEAD_DIM
    return (owner == lax.broadcasted_iota(jnp.int32, (MIXER_HEADS, INNER), 0)).astype(f32)


def per_channel(value):
    return jnp.dot(value, head_map(), precision=highest)


def per_head(value):
    return lax.dot_general(
        value, head_map(), (((1,), (1,)), ((), ())), precision=highest, preferred_element_type=f32
    )


def bit_plan():
    seq_bits = lax.axis_size("seq").bit_length() - 1
    fsdp_bits = lax.axis_size("fsdp").bit_length() - 1
    dims = [("seq", bit) for bit in reversed(range(seq_bits))]
    dims += [("fsdp", bit) for bit in reversed(range(fsdp_bits))]
    middle = [("seq", bit) for bit in range(1, seq_bits)]
    last = [("fsdp", bit) for bit in range(fsdp_bits)]
    orders = [
        [dims.index(step) for step in [("seq", 0)] + middle + last],
        [dims.index(step) for step in [("seq", 0)] + middle[::-1] + last],
    ]
    return dims, orders


def kernels_fit(rows):
    seq, fsdp = lax.axis_size("seq"), lax.axis_size("fsdp")
    return rows % 8 == 0 and rows >= 64 and seq > 1 and seq & (seq - 1) == 0 and fsdp & (fsdp - 1) == 0


def row_streams(rows, parts):
    tiles = rows // 16
    edges = [16 * (tiles * part // parts) for part in range(parts)] + [rows]
    return list(zip(edges[:-1], edges[1:]))


def my_bits(dims):
    index = {axis: lax.axis_index(axis) for axis in ("seq", "fsdp")}
    return [(index[axis] // (1 << bit)) % 2 for axis, bit in dims], index


def partner_of(dims, index, bits, dim):
    axis, bit = dims[dim]
    return {axis: index[axis] + (1 - 2 * bits[dim]) * (1 << bit)}


def greet(dims, index, bits):
    barrier = pltpu.get_barrier_semaphore()
    for dim in range(len(dims)):
        pl.semaphore_signal(
            barrier, inc=1, device_id=partner_of(dims, index, bits, dim),
            device_id_type=pl.DeviceIdType.MESH,
        )
    pl.semaphore_wait(barrier, len(dims))


def scatter_sum(parts, rows):
    dims, orders = bit_plan()
    depth = len(dims)
    streams = row_streams(rows, 4)
    blocks = lax.axis_size("seq") * lax.axis_size("fsdp")
    copies = []
    start = 0
    for which, part in enumerate(parts):
        row = 0
        while row < part.shape[0]:
            block, inner = divmod(start + row, rows)
            size = min(rows - inner, part.shape[0] - row)
            copies.append((which, row, block, inner, size))
            row += size
        start += part.shape[0]
    assert start == blocks * rows

    def kernel(*refs):
        sources = refs[: len(parts)]
        out_ref, work, local_sem, send_sem, recv_sem = refs[len(parts) : len(parts) + 5]
        landing = refs[len(parts) + 5 :]
        bits, index = my_bits(dims)
        local = []
        for at, (which, row, block, inner, size) in enumerate(copies):
            where = tuple((block >> (depth - 1 - dim)) % 2 for dim in range(depth))
            copy = pltpu.make_async_copy(
                sources[which].at[pl.ds(row, size)],
                work.at[where + (pl.ds(inner, size),)],
                local_sem.at[at],
            )
            copy.start()
            local.append(copy)
        greet(dims, index, bits)
        for copy in local:
            copy.wait()
        sent = []

        def region(stream, stage, flip):
            first, last = streams[stream]
            order = orders[stream % 2]
            where = [slice(None)] * depth
            for dim in order[:stage]:
                where[dim] = bits[dim]
            where[order[stage]] = 1 - bits[order[stage]] if flip else bits[order[stage]]
            return where, pl.ds(first, last - first)

        def take(stream, stage):
            sent[stage * len(streams) + stream].wait_recv()
            arrived = landing[stage * len(streams) + stream]
            where, lines = region(stream, stage, False)
            free = [dim for dim in range(depth) if isinstance(where[dim], slice)]
            for choice in itertools.product(range(2), repeat=len(free)):
                spot = list(where)
                for dim, value in zip(free, choice):
                    spot[dim] = value
                total = work[tuple(spot) + (lines,)].astype(f32) + arrived[choice].astype(f32)
                if stage == depth - 1:
                    out_ref[lines] = total.astype(bf16)
                else:
                    work[tuple(spot) + (lines,)] = total.astype(bf16)

        for stage in range(depth):
            for stream in range(len(streams)):
                if stage > 0:
                    take(stream, stage - 1)
                where, lines = region(stream, stage, True)
                slot = stage * len(streams) + stream
                copy = pltpu.make_async_remote_copy(
                    src_ref=work.at[tuple(where) + (lines,)],
                    dst_ref=landing[slot],
                    send_sem=send_sem.at[slot],
                    recv_sem=recv_sem.at[slot],
                    device_id=partner_of(dims, index, bits, orders[stream % 2][stage]),
                    device_id_type=pl.DeviceIdType.MESH,
                )
                copy.start()
                sent.append(copy)
        for stream in range(len(streams)):
            take(stream, depth - 1)
        for copy in sent:
            copy.wait_send()

    slots = depth * len(streams)
    buffers = [
        pltpu.VMEM((2,) * (depth - 1 - stage) + (last - first, LANES), bf16)
        for stage in range(depth)
        for first, last in streams
    ]
    return pl.pallas_call(
        kernel,
        out_shape=jax.ShapeDtypeStruct((rows, LANES), bf16),
        in_specs=[pl.BlockSpec(memory_space=pl.ANY)] * len(parts),
        out_specs=pl.BlockSpec(memory_space=pltpu.VMEM),
        scratch_shapes=[
            pltpu.VMEM((2,) * depth + (rows, LANES), bf16),
            pltpu.SemaphoreType.DMA((len(copies),)),
            pltpu.SemaphoreType.DMA((slots,)),
            pltpu.SemaphoreType.DMA((slots,)),
        ] + buffers,
        compiler_params=pltpu.CompilerParams(
            collective_id=0, has_side_effects=True, vmem_limit_bytes=40 * 2**20
        ),
        name="scatter_sum",
    )(*parts)


def gather_all(shard):
    dims, orders = bit_plan()
    orders = [order[::-1] for order in orders]
    depth = len(dims)
    rows = shard.shape[0]
    streams = row_streams(rows, 4)

    def kernel(shard_ref, out_ref, local_sem, send_sem, recv_sem):
        bits, index = my_bits(dims)
        own = pltpu.make_async_copy(shard_ref, out_ref.at[tuple(bits)], local_sem)
        own.start()
        greet(dims, index, bits)
        own.wait()
        sent = []
        for stage in range(depth):
            for stream, (first, last) in enumerate(streams):
                order = orders[stream % 2]
                if stage > 0:
                    sent[(stage - 1) * len(streams) + stream].wait_recv()
                where = list(bits)
                for dim in order[:stage]:
                    where[dim] = slice(None)
                area = out_ref.at[tuple(where) + (pl.ds(first, last - first),)]
                slot = stage * len(streams) + stream
                copy = pltpu.make_async_remote_copy(
                    src_ref=area,
                    dst_ref=area,
                    send_sem=send_sem.at[slot],
                    recv_sem=recv_sem.at[slot],
                    device_id=partner_of(dims, index, bits, order[stage]),
                    device_id_type=pl.DeviceIdType.MESH,
                )
                copy.start()
                sent.append(copy)
        for copy in sent[-len(streams) :]:
            copy.wait_recv()
        for copy in sent:
            copy.wait_send()

    slots = depth * len(streams)
    whole = pl.pallas_call(
        kernel,
        out_shape=jax.ShapeDtypeStruct((2,) * depth + (rows, LANES), bf16),
        in_specs=[pl.BlockSpec(memory_space=pltpu.VMEM)],
        out_specs=pl.BlockSpec(memory_space=pl.ANY),
        scratch_shapes=[
            pltpu.SemaphoreType.DMA,
            pltpu.SemaphoreType.DMA((slots,)),
            pltpu.SemaphoreType.DMA((slots,)),
        ],
        compiler_params=pltpu.CompilerParams(collective_id=1, has_side_effects=True),
        name="gather_all",
    )(shard)
    return whole.reshape(-1, LANES)


def body(block_input, out_grad, params, first_moment, second_moment):
    shard_half = params.astype(bf16).reshape(-1, LANES)
    if kernels_fit(shard_half.shape[0]):
        whole_half = gather_all(shard_half)
    else:
        whole_half = lax.all_gather(shard_half, ("seq", "fsdp"), axis=0, tiled=True)
    sizes = [MODEL_WIDTH * PROJ, INNER * MODEL_WIDTH, KERNEL * CHANNELS, CHANNELS, MODEL_WIDTH, INNER]
    pieces = []
    row = 0
    for size in sizes:
        pieces.append(whole_half[row : row + size // LANES])
        row = row + size // LANES
    in_weight = pieces[0].reshape(MODEL_WIDTH, PROJ)
    out_weight = pieces[1].reshape(INNER, MODEL_WIDTH)
    conv_weight = pieces[2].astype(f32).reshape(KERNEL, CHANNELS)
    conv_bias = pieces[3].astype(f32).reshape(-1)
    gain_input = pieces[4].astype(f32).reshape(-1)
    gain_gated = pieces[5].astype(f32).reshape(-1)
    small = whole_half[row : row + 1].astype(f32).reshape(-1)
    dt_bias = small[:MIXER_HEADS]
    a_log = small[MIXER_HEADS : 2 * MIXER_HEADS]
    skip_gain = small[2 * MIXER_HEADS : 3 * MIXER_HEADS]
    residual = block_input[0].astype(f32)
    cotangent = out_grad[0]
    tokens_dev = residual.shape[0]
    inv_rms = lax.rsqrt(jnp.mean(residual * residual, axis=-1, keepdims=True) + norm_epsilon)
    normed = (residual * inv_rms * gain_input).astype(bf16)
    projected = row_major(jnp.dot(normed, in_weight, preferred_element_type=f32).astype(bf16))
    gate_z = projected[:, :INNER].astype(f32)
    conv_in = projected[:, INNER : INNER + CHANNELS]
    dt_raw = projected[:, INNER + CHANNELS :].astype(f32)
    left_rows = passed_along(conv_in[tokens_dev - KERNEL + 1 :], "seq", 1)
    padded = jnp.concatenate([left_rows, conv_in], 0).astype(f32)
    conv_out = jnp.zeros((tokens_dev, CHANNELS), f32) + conv_bias[None, :]
    for tap_index in range(KERNEL):
        conv_out = (
            conv_out + conv_weight[tap_index][None, :] * padded[tap_index : tap_index + tokens_dev]
        )
    activated = row_major(jax.nn.silu(conv_out).astype(bf16))
    x_half = activated[:, :INNER]
    b_half = activated[:, INNER : INNER + STATE]
    c_half = activated[:, INNER + STATE :]
    values = x_half.astype(f32)
    pre_dt = dt_raw + dt_bias[None, :]
    steps_dt = jax.nn.softplus(pre_dt)
    a_rate = -jnp.exp(a_log)
    log_decay = steps_dt * a_rate[None, :]
    causal = jnp.arange(tokens_dev)[:, None] >= jnp.arange(tokens_dev)[None, :]
    triangle = causal.astype(f32)
    cumulative = jnp.dot(triangle, log_decay, precision=highest)
    segment_log = cumulative[-1]
    cum_t, dt_t = cumulative.T, steps_dt.T
    cum_wide = jnp.pad(cumulative, ((0, 0), (0, LANES - MIXER_HEADS)))
    to_end = jnp.exp(segment_log[None, :] - cumulative)
    from_start = jnp.exp(cumulative)
    tail_weight = per_channel(to_end * steps_dt)
    head_weight = per_channel(from_start)
    x_tail = (values * tail_weight).astype(bf16)
    local_state = dot_atb(x_tail, b_half).astype(bf16)
    log_high = lax.reduce_precision(segment_log, 8, 7)
    log_rows = jnp.concatenate(
        [log_high, segment_log - log_high, jnp.zeros((LANES - 2 * MIXER_HEADS,), f32)]
    )
    log_rows = jnp.pad(log_rows[None, :], ((0, 15), (0, 0))).astype(bf16)
    count, mine = lax.axis_size("seq"), lax.axis_index("seq")
    gathered = lax.all_gather(jnp.concatenate([local_state, log_rows], 0), "seq")
    y_inside = inside_forward(x_half, b_half, c_half, cum_wide, cum_t, dt_t)
    logs = gathered[:, INNER].astype(f32)
    logs = logs[:, :MIXER_HEADS] + logs[:, MIXER_HEADS : 2 * MIXER_HEADS]
    source = jnp.arange(count)
    between = (source[None, :] > source[:, None]) & (source[None, :] < mine)
    earlier = jnp.exp(jnp.sum(jnp.where(between[:, :, None], logs[None], 0.0), 1))
    earlier = per_channel(jnp.where(source[:, None] < mine, earlier, 0.0))
    between = (source[None, :] < source[:, None]) & (source[None, :] > mine)
    later = jnp.exp(jnp.sum(jnp.where(between[:, :, None], logs[None], 0.0), 1))
    later = per_channel(jnp.where(source[:, None] > mine, later, 0.0))
    state_in = jnp.sum(gathered[:, :INNER].astype(f32) * earlier[:, :, None], 0)
    state_half = state_in.astype(bf16)
    y_carried = dot_abt(c_half, state_half) * head_weight
    skip_wide = per_channel(skip_gain[None, :])
    y_carried = row_major(y_carried)
    mixed = y_inside + y_carried + skip_wide * values
    gate_act = jax.nn.silu(gate_z)
    gated = mixed * gate_act
    inv_gated = lax.rsqrt(jnp.mean(gated * gated, axis=-1, keepdims=True) + norm_epsilon)
    normed_out = (gated * inv_gated * gain_gated).astype(bf16)
    output = residual + jnp.dot(normed_out, out_weight, preferred_element_type=f32)
    d_out_weight = dot_atb(normed_out, cotangent).astype(bf16)
    d_normed_out = row_major(dot_abt(cotangent, out_weight))
    d_gain_gated = jnp.sum(d_normed_out * gated * inv_gated, 0)
    scaled_grad = d_normed_out * gain_gated
    d_gated = inv_gated * scaled_grad - gated * inv_gated**3 * jnp.mean(
        scaled_grad * gated, axis=-1, keepdims=True
    )
    d_mixed = d_gated * gate_act
    d_gate_z = d_gated * mixed * silu_grad(gate_z)
    d_skip = per_head(jnp.sum(d_mixed * values, 0)[None, :])[0]
    dy_half = row_major(d_mixed.astype(bf16))
    dy_head = (d_mixed * head_weight).astype(bf16)
    local_grad = dot_atb(dy_head, c_half).astype(bf16)
    gathered_grad = lax.all_gather(local_grad, "seq")
    dx_inside, db_inside, dc_inside, row_mass, col_mass = inside_backward(
        x_half, dy_half, b_half, c_half, cum_wide, cum_t, dt_t
    )
    later_grad = jnp.sum(gathered_grad.astype(f32) * later[:, :, None], 0)
    grad_half = later_grad.astype(bf16)
    bg = row_major(dot_abt(b_half, grad_half))
    d_values = dx_inside + tail_weight * bg + skip_wide * d_mixed
    d_inputs_b = db_inside + dot_ab(x_tail, grad_half)
    d_outputs_c = dc_inside + dot_ab(dy_head, state_half)
    tail_mass = per_head(values * bg) * to_end
    d_steps_ssd = col_mass.T + tail_mass
    state_mass = per_head(jnp.sum(later_grad * state_in, 1)[None, :])[0]
    d_cumulative = row_mass[:, :MIXER_HEADS] + per_head(d_mixed * y_carried) - steps_dt * d_steps_ssd
    d_last = jnp.sum(steps_dt * tail_mass, 0) + jnp.exp(segment_log) * state_mass
    d_log_decay = d_last[None, :] + lax.dot_general(
        triangle, d_cumulative, (((0,), (0,)), ((), ())), precision=highest
    )
    d_steps = d_steps_ssd + d_log_decay * a_rate[None, :]
    d_a_log = jnp.sum(d_log_decay * steps_dt, 0) * a_rate
    d_pre_dt = d_steps * jax.nn.sigmoid(pre_dt)
    d_dt_bias = jnp.sum(d_pre_dt, 0)
    d_activated = jnp.concatenate([d_values, d_inputs_b, d_outputs_c], 1)
    d_conv_out = row_major(d_activated * silu_grad(conv_out))
    d_conv_bias = jnp.sum(d_conv_out, 0)
    d_conv_weight = jnp.stack(
        [
            jnp.sum(d_conv_out * padded[tap_index : tap_index + tokens_dev], 0)
            for tap_index in range(KERNEL)
        ],
        0,
    )
    d_padded = jnp.zeros((tokens_dev + KERNEL - 1, CHANNELS), jnp.float32)
    for tap_index in range(KERNEL):
        d_padded = d_padded + jnp.pad(
            d_conv_out * conv_weight[tap_index][None, :],
            ((tap_index, KERNEL - 1 - tap_index), (0, 0)),
        )
    right_rows = passed_along(d_padded[: KERNEL - 1], "seq", -1)
    d_conv_in = d_padded[KERNEL - 1 :]
    d_conv_in = jnp.concatenate(
        [d_conv_in[: tokens_dev - KERNEL + 1], d_conv_in[tokens_dev - KERNEL + 1 :] + right_rows], 0
    )
    d_projected = row_major(jnp.concatenate([d_gate_z, d_conv_in, d_pre_dt], 1).astype(bf16))
    d_in_weight = row_major(dot_atb(normed, d_projected).astype(bf16))
    d_normed = jnp.dot(d_projected, in_weight.T, preferred_element_type=jnp.float32)
    d_gain_input = jnp.sum(d_normed * residual * inv_rms, 0)
    scaled_in = d_normed * gain_input
    d_residual = inv_rms * scaled_in - residual * inv_rms**3 * jnp.mean(
        scaled_in * residual, axis=-1, keepdims=True
    )
    input_grad = cotangent.astype(jnp.float32) + d_residual
    tail_vector = jnp.concatenate(
        [d_dt_bias, d_a_log, d_skip, jnp.zeros((PARAMS - RAW,), f32)]
    )
    small_parts = [d_conv_weight, d_conv_bias, d_gain_input, d_gain_gated, tail_vector]
    small_rows = jnp.concatenate([part.astype(bf16).reshape(-1, LANES) for part in small_parts], 0)
    parts = [d_in_weight.astype(bf16).reshape(-1, LANES), d_out_weight.reshape(-1, LANES), small_rows]
    if kernels_fit(shard_half.shape[0]):
        grad_shard = scatter_sum(parts, shard_half.shape[0])
    else:
        flat_local = jnp.concatenate(parts, 0)
        grad_shard = lax.psum_scatter(flat_local, ("seq", "fsdp"), scatter_dimension=0, tiled=True)
    grad_shard = grad_shard.reshape(-1).astype(f32)
    new_params, new_first, new_second = adam_update(params, grad_shard, first_moment, second_moment)
    return (output[None], input_grad[None], grad_shard, new_params, new_first, new_second)


def solution(mesh):
    return jax.shard_map(
        body,
        mesh=mesh,
        in_specs=(
            P("fsdp", "seq", None),
            P("fsdp", "seq", None),
            P(("seq", "fsdp")),
            P(("seq", "fsdp")),
            P(("seq", "fsdp")),
        ),
        out_specs=(
            P("fsdp", "seq", None),
            P("fsdp", "seq", None),
            P(("seq", "fsdp")),
            P(("seq", "fsdp")),
            P(("seq", "fsdp")),
            P(("seq", "fsdp")),
        ),
        check_vma=False,
    )
```

profile of v0, /device:TPU:0, one launch (start us, length us, event | category | flops | bytes accessed | tf_op | source)
XLA Modules:
  0.0 300.6 jit_solution(13347616849981505765)
XLA Ops:
  7.2 1.7 convert_bitcast_fusion.1.shard_ref
  8.9 56.6 %gather_all.1 = bf16[2,2,2,2,2,920,128]{6,5,4,3,2,1,0:T(8,128)(2,1)} custom-call(bf16[920,128]{1,0:T(8,128)(2,1)} %convert_bitcast_fusion.1.shard_ref), custom_call_target="tpu_custom_call" | custom-call | tf_op jit(solution)/shard_map/gather_all/pallas_call | solution.py:396
  66.3 5.8 %slice.161 = bf16[20112,128]{1,0:T(8,128)(2,1)} slice(bf16[29440,128]{1,0:T(8,128)(2,1)} %bitcast.141), slice={[0:20112], [0:128]} | slice | bytes 10297344 | tf_op jit(solution)/shard_map/slice | solution.py:422
  72.8 10.4 %reshape.213 = bf16[768,3352]{1,0:T(8,128)(2,1)} reshape(bf16[20112,128]{1,0:T(8,128)(2,1)} %slice.161) | data formatting | bytes 10297344 | tf_op jit(solution)/shard_map/reshape | solution.py:424
  83.2 4.2 %convolution_convert_fusion.1 = bf16[256,3352]{1,0:T(8,128)(2,1)S(1)} fusion(bf16[768,3352]{1,0:T(8,128)(2,1)} %reshape.213, bf16[1,256,768]{2,1,0:T(8,128)(2,1)S(1)} %copy-done.24, f32[768]{0:T(1024)S(1)} %fusion.112, f32[256]{0:T(256)S(1)} %get-tuple-element.57), kind=kOutput, calls=%fused_computation.4 | convolution fusion | flops 1319704576 | bytes 7262208 | tf_op jit(solution)/shard_map/dot_general | solution.py:439
  87.4 2.3 collective-permute-start
  93.8 2.4 multiply_convert_fusion
  97.8 1.7 slice.182
  99.5 3.2 %reshape.215 = bf16[1536,768]{1,0:T(8,128)(2,1)} reshape(bf16[9216,128]{1,0:T(8,128)(2,1)S(1)} %slice.182) | data formatting | bytes 4718592 | tf_op jit(solution)/shard_map/reshape | solution.py:425
  103.4 0.9 fusion.128
  105.0 0.9 convolution_reduce_fusion
  106.6 2.0 fusion.65
  108.6 0.9 slice.171.x_ref
  110.2 6.5 %inside_forward.1 = f32[256,1536]{1,0:T(8,128)} custom-call(bf16[256,1536]{1,0:T(8,128)(2,1)} %slice.171.x_ref, bf16[256,128]{1,0:T(8,128)(2,1)} %get-tuple-element.49.b_ref, bf16[256,128]{1,0:T(8,128)(2,1)} %get-tuple-element.48.c_ref, f32[256,128]{1,0:T(8,128)} %pad.25.cum_ref, f32[24,256]{1,0:T(8,128)} %bitcast.151, f32[24,256]{1,0:T(8,128)} %copy.46.dt_t_ref), custom_call_target="tpu_custom_call" | custom-call | flops 402653184 | bytes 1572864 | tf_op jit(solution)/shard_map/inside_forward/pallas_call | solution.py:150
  116.7 13.2 %all-gather.5.cloned.1.call-done = bf16[12416,128]{1,0:T(8,128)(2,1)} async-done(((bf16[1552,128]{1,0:T(8,128)(2,1)}), bf16[12416,128]{1,0:T(8,128)(2,1)}) %all-gather.5.cloned.1.call-update) | async-done | bytes 3178512 | tf_op jit(solution)/shard_map/all_gather | solution.py:477
  131.1 4.0 %multiply_reduce_fusion = f32[1536,128]{1,0:T(8,128)S(1)} fusion(bf16[8,1552,128]{2,1,0:T(8,128)(2,1)} %bitcast.150, f32[8,1536]{1,0:T(8,128)S(1)} %fusion.66), kind=kLoop, calls=%fused_computation.3 | loop fusion | flops 4521984 | bytes 3981312 | tf_op jit(solution)/shard_map/reduce_sum | solution.py:488
  135.1 2.7 multiply_reduce_fusion.7
  138.0 1.5 multiply_reduce_fusion.5
  139.5 1.0 copy-done.31
  140.4 2.4 fusion.11
  142.9 1.4 multiply_convert_fusion.1
  144.3 1.2 convolution_convert_fusion.3
  145.5 9.2 %inside_backward.1 = (f32[256,1536]{1,0:T(8,128)}, f32[256,128]{1,0:T(8,128)}, f32[256,128]{1,0:T(8,128)}, f32[256,128]{1,0:T(8,128)}, f32[24,256]{1,0:T(8,128)}) custom-call(bf16[256,1536]{1,0:T(8,128)(2,1)} %slice.171.x_ref, bf16[256,1536]{1,0:T(8,128)(2,1)} %get-tuple-element.47.dy_ref, bf16[256,128]{1,0:T(8,128)(2,1)} %get-tuple-element.49.b_ref, ...), custom_call_target="tpu_custom_call" | custom-call | flops 805306368 | bytes 3145728 | tf_op jit(solution)/shard_map/inside_backward/pallas_call | solution.py:166
  154.7 1.5 copy.52
  156.2 3.3 %convolution_convert_fusion.2 = bf16[1536,768]{1,0:T(8,128)(2,1)} fusion(bf16[1,256,768]{2,1,0:T(8,128)(2,1)} %param.6, f32[256,1536]{1,0:T(8,128)S(1)} %get-tuple-element.37, f32[1536]{0:T(1024)S(1)} %fusion.104, f32[256]{0:T(256)S(1)} %get-tuple-element.59), kind=kOutput, calls=%fused_computation.5 | convolution fusion | flops 606339072 | bytes 4332544 | tf_op jit(solution)/shard_map/dot_general | solution.py:70
  159.5 4.2 %reshape.217.refs_1_ = bf16[9216,128]{1,0:T(8,128)(2,1)S(1)} reshape(bf16[1536,768]{1,0:T(8,128)(2,1)} %convolution_convert_fusion.2) | data formatting | bytes 4718592 | tf_op jit(solution)/shard_map/reshape | solution.py:569
  164.5 0.8 fusion.64
  165.3 2.0 convolution_add_fusion.2
  167.4 3.4 %fusion.14 = f32[1,256,768]{2,1,0:T(8,128)} fusion(bf16[1536,768]{1,0:T(8,128)(2,1)} %reshape.215, bf16[1,256,768]{2,1,0:T(8,128)(2,1)S(1)} %copy-done.25, f32[256,1536]{1,0:T(8,128)S(1)} %copy-done.10, f32[1536]{0:T(1024)S(1)} %fusion.104, f32[256]{0:T(256)S(1)} %copy-done.51), kind=kOutput, calls=%fused_computation.48 | convolution fusion | flops 605552640 | bytes 5118976 | tf_op jit(solution)/shard_map/dot_general | solution.py:498
  170.8 7.2 %all-gather.7.cloned.1.call-done = bf16[12288,128]{1,0:T(8,128)(2,1)} async-done(((bf16[1536,128]{1,0:T(8,128)(2,1)}), bf16[12288,128]{1,0:T(8,128)(2,1)}) %all-gather.7.cloned.1.call-update) | async-done | bytes 3145744 | tf_op jit(solution)/shard_map/all_gather | solution.py:512
  178.0 4.0 %fusion = f32[1536,128]{1,0:T(8,128)S(1)} fusion(bf16[8,1536,128]{2,1,0:T(8,128)(2,1)} %bitcast.148, f32[8,1536]{1,0:T(8,128)} %fusion.64), kind=kLoop, calls=%fused_computation.2 | loop fusion | flops 4521984 | bytes 3981312 | tf_op jit(solution)/shard_map/reduce_sum | solution.py:516
  182.7 1.0 copy-done.8
  184.7 1.0 copy-done.2
  186.3 2.4 multiply_reduce_fusion.4
  192.2 1.5 pad_add_fusion
  193.8 1.9 multiply_reduce_fusion.10
  195.8 1.3 collective-permute-start.1
  197.3 1.8 fusion.19
  199.2 1.2 fusion.134
  200.6 1.1 slice.270
  201.9 1.1 fusion.99
  203.4 5.1 %fusion.40 = (bf16[768]{0:T(1024)(128)(2,1)S(1)}, f32[256]{0:T(256)S(1)}, f32[256,768]{1,0:T(8,128)}) fusion(bf16[1,256,768]{2,1,0:T(8,128)(2,1)S(1)} %copy-done.26, f32[256]{0:T(256)S(1)} %copy-done.65, f32[768]{0:T(1024)S(1)} %copy-done.57, bf16[768,3352]{1,0:T(8,128)(2,1)} %reshape.213, bf16[256,24]{1,0:T(8,128)(2,1)S(1)} %get-tuple-element.34, ...), kind=kOutput, calls=%fused_computation.84 | convolution fusion | flops 1326300160 | bytes 8051200 | tf_op jit(solution)/shard_map/dot_general | solution.py:557
  208.5 4.0 %convolution_convert_fusion = bf16[768,3352]{1,0:T(8,128)(2,1)} fusion(bf16[1,256,768]{2,1,0:T(8,128)(2,1)S(1)} %copy-done.26, f32[768]{0:T(1024)S(1)} %copy-done.57, f32[256]{0:T(256)S(1)} %copy-done.65, bf16[256,24]{1,0:T(8,128)(2,1)S(1)} %get-tuple-element.34, bf16[3,1792]{1,0:T(4,128)(2,1)S(1)} %fusion.99, bf16[253,1792]{1,0:T(8,128)(2,1)S(1)} %copy-done.32, ...), kind=kOutput, calls=%fused_computation | convolution fusion | flops 1328285696 | bytes 7262208 | tf_op jit(solution)/shard_map/dot_general | solution.py:70
  212.6 10.3 %reshape.216.refs_0_ = bf16[20112,128]{1,0:T(8,128)(2,1)} reshape(bf16[768,3352]{1,0:T(8,128)(2,1)} %convolution_convert_fusion) | data formatting | bytes 10297344 | tf_op jit(solution)/shard_map/reshape | solution.py:569
  222.9 2.3 fusion.35
  225.4 2.5 copy-done
  227.8 64.5 %scatter_sum.1 = bf16[920,128]{1,0:T(8,128)(2,1)S(1)} custom-call(bf16[20112,128]{1,0:T(8,128)(2,1)S(1)} %copy-done, bf16[9216,128]{1,0:T(8,128)(2,1)S(1)} %reshape.217.refs_1_, bf16[112,128]{1,0:T(8,128)(2,1)S(1)} %concatenate.35.refs_2_), custom_call_target="tpu_custom_call" | custom-call | tf_op jit(solution)/shard_map/scatter_sum/pallas_call | solution.py:338
  292.4 1.3 multiply_subtract_fusion.1
  (203 shorter events, 18.5 us)
Async XLA Ops:
  7.2 122.8 %all-gather.5.cloned.1.call-start = ((), (), s32[]{:S(2)}) async-start(), calls=%async_computation | async-start | bytes 3575808 | tf_op jit(solution)/shard_map/all_gather | solution.py:477
  66.3 17.0 %copy-start.56 = (f32[768]{0:T(1024)}, f32[768]{0:T(1024)S(1)}, u32[]{:S(2)}) copy-start(f32[768]{0:T(1024)S(1)} %fusion.112) | copy-start | bytes 9220
  66.3 5.8 %copy-start.24 = (bf16[1,256,768]{2,1,0:T(8,128)(2,1)S(1)}, bf16[1,256,768]{2,1,0:T(8,128)(2,1)}, u32[]{:S(2)}) copy-start(bf16[1,256,768]{2,1,0:T(8,128)(2,1)} %param.5) | copy-start | bytes 1179652
  72.8 10.5 %copy-start.64 = (f32[256]{0:T(256)}, f32[256]{0:T(256)S(1)}, u32[]{:S(2)}) copy-start(f32[256]{0:T(256)S(1)} %get-tuple-element.57) | copy-start | bytes 3076
  87.4 6.1 %copy-start.27 = (bf16[256,3352]{1,0:T(8,128)(2,1)}, bf16[256,3352]{1,0:T(8,128)(2,1)S(1)}, u32[]{:S(2)}) copy-start(bf16[256,3352]{1,0:T(8,128)(2,1)S(1)} %convolution_convert_fusion.1) | copy-start | bytes 5148676
  87.4 6.1 %collective-permute-start = (bf16[3,1792]{1,0:T(4,128)(2,1)S(1)}, bf16[3,1792]{1,0:T(4,128)(2,1)S(1)}, u32[]{:S(2)}, u32[]{:S(2)}) collective-permute-start(bf16[3,1792]{1,0:T(4,128)(2,1)S(1)} %slice.162), channel_id=1, source_target_pairs={{0,4},{4,8},{8,12},{12,16},{16,20},{20,24},{24,28},{1,5},{5,9},{9,... | collective-permute-start | bytes 32264 | tf_op jit(solution)/shard_map/ppermute | solution.py:37
  89.8 74.7 %copy-start.52 = (pred[1536]{0:T(1024)(128)(4,1)}, pred[1536]{0:T(1024)(128)(4,1)S(1)}, u32[]{:S(2)}) copy-start(pred[1536]{0:T(1024)(128)(4,1)S(1)} %fusion.103) | copy-start | bytes 4612
  89.8 74.7 %copy-start.37 = (s32[1536]{0:T(1024)}, s32[1536]{0:T(1024)S(1)}, u32[]{:S(2)}) copy-start(s32[1536]{0:T(1024)S(1)} %get-tuple-element.70) | copy-start | bytes 18436
  92.3 14.3 %copy-start.41 = (f32[256,24]{0,1:T(8,128)}, f32[256,24]{0,1:T(8,128)S(1)}, u32[]{:S(2)}) copy-start(f32[256,24]{0,1:T(8,128)S(1)} %fusion.58) | copy-start | bytes 73732
  93.4 2.9 copy-start.11
  93.8 2.5 copy-start.1
  97.5 80.5 %all-gather.7.cloned.1.call-start = ((), (), s32[]{:S(2)}) async-start(), calls=%async_computation.1 | async-start | bytes 3538944 | tf_op jit(solution)/shard_map/all_gather | solution.py:512
  99.5 3.9 %copy-start.61 = (f32[24]{0:T(128)S(1)}, f32[24]{0:T(128)}, u32[]{:S(2)}) copy-start(f32[24]{0:T(128)} %copy-done.60) | copy-start | bytes 292
  105.9 33.6 %copy-start.54 = (f32[1536]{0:T(1024)}, f32[1536]{0:T(1024)S(1)}, u32[]{:S(2)}) copy-start(f32[1536]{0:T(1024)S(1)} %convolution_reduce_fusion) | copy-start | bytes 18436
  131.1 4.0 %copy-start.20 = (f32[256,1536]{1,0:T(8,128)S(1)}, f32[256,1536]{1,0:T(8,128)}, u32[]{:S(2)}) copy-start(f32[256,1536]{1,0:T(8,128)} %fusion.65) | copy-start | bytes 4718596
  131.1 4.0 %copy-start.28 = (bf16[256,3352]{1,0:T(8,128)(2,1)S(1)}, bf16[256,3352]{1,0:T(8,128)(2,1)}, u32[]{:S(2)}) copy-start(bf16[256,3352]{1,0:T(8,128)(2,1)} %copy-done.27) | copy-start | bytes 5148676
  135.1 2.8 copy-start.16
  135.1 2.8 copy-start.13
  135.1 2.8 copy-start.22
  137.9 18.3 %copy-start.9 = (f32[256,1536]{1,0:T(8,128)}, f32[256,1536]{1,0:T(8,128)S(1)}, u32[]{:S(2)}) copy-start(f32[256,1536]{1,0:T(8,128)S(1)} %get-tuple-element.37) | copy-start | bytes 4718596
  137.9 18.3 %copy-start.50 = (f32[256]{0:T(256)}, f32[256]{0:T(256)S(1)}, u32[]{:S(2)}) copy-start(f32[256]{0:T(256)S(1)} %get-tuple-element.59) | copy-start | bytes 3076
  137.9 2.5 copy-start.31
  144.3 10.4 %copy-start.15 = (bf16[256,1536]{1,0:T(8,128)(2,1)}, bf16[256,1536]{1,0:T(8,128)(2,1)S(1)}, u32[]{:S(2)}) copy-start(bf16[256,1536]{1,0:T(8,128)(2,1)S(1)} %get-tuple-element.46) | copy-start | bytes 2359300
  163.7 3.6 %copy-start.10 = (f32[256,1536]{1,0:T(8,128)S(1)}, f32[256,1536]{1,0:T(8,128)}, u32[]{:S(2)}) copy-start(f32[256,1536]{1,0:T(8,128)} %copy-done.9) | copy-start | bytes 4718596
  163.7 3.6 %copy-start.25 = (bf16[1,256,768]{2,1,0:T(8,128)(2,1)S(1)}, bf16[1,256,768]{2,1,0:T(8,128)(2,1)}, u32[]{:S(2)}) copy-start(bf16[1,256,768]{2,1,0:T(8,128)(2,1)} %param.5) | copy-start | bytes 1179652
  163.7 3.6 %copy-start.51 = (f32[256]{0:T(256)S(1)}, f32[256]{0:T(256)}, u32[]{:S(2)}) copy-start(f32[256]{0:T(256)} %copy-done.50) | copy-start | bytes 3076
  178.0 4.0 %copy-start.17 = (f32[1536,128]{1,0:T(8,128)S(1)}, f32[1536,128]{1,0:T(8,128)}, u32[]{:S(2)}) copy-start(f32[1536,128]{1,0:T(8,128)} %copy-done.16) | copy-start | bytes 2359300
  178.0 4.3 %copy-start.12 = (f32[256,1536]{1,0:T(8,128)S(1)}, f32[256,1536]{1,0:T(8,128)}, u32[]{:S(2)}) copy-start(f32[256,1536]{1,0:T(8,128)} %copy-done.11) | copy-start | bytes 4718596
  178.0 4.3 %copy-start.40 = (f32[256,128]{1,0:T(8,128)S(1)}, f32[256,128]{1,0:T(8,128)}, u32[]{:S(2)}) copy-start(f32[256,128]{1,0:T(8,128)} %get-tuple-element.12) | copy-start | bytes 393220
  186.2 2.5 copy-start.43
  186.2 2.5 copy-start.45
  186.3 2.5 copy-start.47
  186.3 2.5 copy-start.49
  189.3 2.4 copy-start.5
  189.3 2.9 copy-start.6
  193.8 3.5 %copy-start.19 = (f32[256,1536]{1,0:T(8,128)S(1)}, f32[256,1536]{1,0:T(8,128)}, u32[]{:S(2)}) copy-start(f32[256,1536]{1,0:T(8,128)} %copy-done.18) | copy-start | bytes 4718596
  193.8 3.5 %copy-start.34 = (f32[24,256]{0,1:T(8,128)S(1)}, f32[24,256]{0,1:T(8,128)}, u32[]{:S(2)}) copy-start(f32[24,256]{0,1:T(8,128)} %copy.52) | copy-start | bytes 73732
  193.8 3.5 %copy-start.39 = (f32[256,128]{1,0:T(8,128)S(1)}, f32[256,128]{1,0:T(8,128)}, u32[]{:S(2)}) copy-start(f32[256,128]{1,0:T(8,128)} %get-tuple-element.15) | copy-start | bytes 393220
  195.8 6.1 %collective-permute-start.1 = (f32[3,1792]{1,0:T(4,128)}, f32[3,1792]{1,0:T(4,128)}, u32[]{:S(2)}, u32[]{:S(2)}) collective-permute-start(f32[3,1792]{1,0:T(4,128)} %pad_add_fusion.1), channel_id=1, source_target_pairs={{4,0},{8,4},{12,8},{16,12},{20,16},{24,20},{28,24},{5,1},{9,5},{13... | collective-permute-start | bytes 64520 | tf_op jit(solution)/shard_map/ppermute | solution.py:37
  197.3 3.2 %copy-start.67 = (f32[1,128]{1,0:T(1,128)S(1)}, f32[1,128]{1,0:T(1,128)}, u32[]{:S(2)}) copy-start(f32[1,128]{1,0:T(1,128)} %copy-done.66) | copy-start | bytes 1540
  197.3 3.3 %copy-start.21 = (bf16[259,1792]{1,0:T(8,128)(2,1)S(1)}, bf16[259,1792]{1,0:T(8,128)(2,1)}, u32[]{:S(2)}) copy-start(bf16[259,1792]{1,0:T(8,128)(2,1)} %pad_add_fusion) | copy-start | bytes 2784772
  199.2 2.6 copy-start.70
  212.6 10.3 %copy-start.23 = (bf16[1,256,768]{2,1,0:T(8,128)(2,1)S(1)}, bf16[1,256,768]{2,1,0:T(8,128)(2,1)}, u32[]{:S(2)}) copy-start(bf16[1,256,768]{2,1,0:T(8,128)(2,1)} %param.6) | copy-start | bytes 1179652
  212.6 10.3 %copy-start.63 = (f32[256]{0:T(256)S(1)}, f32[256]{0:T(256)}, u32[]{:S(2)}) copy-start(f32[256]{0:T(256)} %get-tuple-element.56) | copy-start | bytes 3076
  225.4 2.5 copy-start
  227.8 64.5 %copy-start.29 = (f32[117760]{0:T(1024)S(1)}, f32[117760]{0:T(1024)}, u32[]{:S(2)}) copy-start(f32[117760]{0:T(1024)} %param.7) | copy-start | bytes 1413124
  227.8 64.5 %copy-start.35 = (f32[117760]{0:T(1024)S(1)}, f32[117760]{0:T(1024)}, u32[]{:S(2)}) copy-start(f32[117760]{0:T(1024)} %param.8) | copy-start | bytes 1413124
  227.8 64.5 %copy-start.36 = (f32[117760]{0:T(1024)S(1)}, f32[117760]{0:T(1024)}, u32[]{:S(2)}) copy-start(f32[117760]{0:T(1024)} %param.9) | copy-start | bytes 1413124
  (29 other events, 44.7 us)
Sparse Core Ops, SparseCore 0:
  97.6 32.2 all-gather.4
  145.6 32.3 all-gather.6
where the time goes:
time: 302 us; the launch traced here: 301 us
  Pallas kernels  137 us (45%)
  local copies, waits for them, and re-layouts  51.2 us (17%)
  matrix products  39.7 us (13%)
  other arithmetic  33.6 us (11%)
  waiting for transfers between devices  20.5 us (7%)
  between operations  15 us (5%)
  starting transfers between devices  3.86 us (1%)
    pallas_call x1, Pallas kernels, scatter_sum(): pl.pallas_call(kernel, out_shape=jax.ShapeDtypeStruct((rows, LANES), bf16...  64.5 us
    pallas_call x1, Pallas kernels, gather_all(): pl.pallas_call(kernel, out_shape=jax.ShapeDtypeStruct((2,) * depth + (row...  56.6 us
    all_gather x1, waiting for transfers between devices, body(): lax.all_gather(jnp.concatenate([local_state, log_rows], 0), 'seq')  13.2 us
    reshape x1, local copies, waits for them, and re-layouts, body(): in_weight = pieces[0].reshape(MODEL_WIDTH, PROJ)  10.4 us
    reshape x1, local copies, waits for them, and re-layouts, body(): d_in_weight.astype(bf16).reshape(-1, LANES)  10.3 us
    unnamed x146, local copies, waits for them, and re-layouts  9.45 us
    pallas_call x1, Pallas kernels, inside_backward(): pl.pallas_call(inside_grad_kernel, out_shape=(jax.ShapeDtypeStruct((token...  9.17 us
    dot_general x4, matrix products, dot_atb(): lax.dot_general(a, b, (((0,), (0,)), ((), ())), preferred_element_type=f32)  8.98 us
  transfers between devices with their start and end apart: 4, of which 2 were waited for; matrix products, arithmetic and copies ran while one was open for 12% of the time, Pallas kernels for 5%

commit v1 on v0

--- a/solution.py
+++ b/solution.py
@@ -250,7 +250,7 @@
 def scatter_sum(parts, rows):
     dims, orders = bit_plan()
     depth = len(dims)
-    streams = row_streams(rows, 4)
+    streams = row_streams(rows, 6)
     blocks = lax.axis_size("seq") * lax.axis_size("fsdp")
     copies = []
     start = 0
@@ -358,7 +358,7 @@
     orders = [order[::-1] for order in orders]
     depth = len(dims)
     rows = shard.shape[0]
-    streams = row_streams(rows, 4)
+    streams = row_streams(rows, 8)
 
     def kernel(shard_ref, out_ref, local_sem, send_sem, recv_sem):
         bits, index = my_bits(dims)

time: 302 us -> 298 us (0.987)
  Pallas kernels: 137 us -> 133 us
    pallas_call x1, Pallas kernels: 56.6 us -> 53.1 us  [gather_all(): pl.pallas_call(kernel, out_shape=jax.ShapeDtypeStruct((2,) * depth + (row...]
where the time goes in v1:
time: 298 us; the launch traced here: 296 us
  Pallas kernels  133 us (45%)
  local copies, waits for them, and re-layouts  51.2 us (17%)
  matrix products  39.8 us (13%)
  other arithmetic  33.6 us (11%)
  waiting for transfers between devices  20.6 us (7%)
  between operations  15 us (5%)
  starting transfers between devices  3.89 us (1%)
    pallas_call x1, Pallas kernels, scatter_sum(): pl.pallas_call(kernel, out_shape=jax.ShapeDtypeStruct((rows, LANES), bf16...  63.7 us
    pallas_call x1, Pallas kernels, gather_all(): pl.pallas_call(kernel, out_shape=jax.ShapeDtypeStruct((2,) * depth + (row...  53.1 us
    all_gather x1, waiting for transfers between devices, body(): lax.all_gather(jnp.concatenate([local_state, log_rows], 0), 'seq')  13.4 us
    reshape x1, local copies, waits for them, and re-layouts, body(): in_weight = pieces[0].reshape(MODEL_WIDTH, PROJ)  10.4 us
    reshape x1, local copies, waits for them, and re-layouts, body(): d_in_weight.astype(bf16).reshape(-1, LANES)  10.3 us
    unnamed x146, local copies, waits for them, and re-layouts  9.45 us
    pallas_call x1, Pallas kernels, inside_backward(): pl.pallas_call(inside_grad_kernel, out_shape=(jax.ShapeDtypeStruct((token...  9.17 us
    dot_general x4, matrix products, dot_atb(): lax.dot_general(a, b, (((0,), (0,)), ((), ())), preferred_element_type=f32)  8.98 us
  transfers between devices with their start and end apart: 4, of which 2 were waited for; matrix products, arithmetic and copies ran while one was open for 12% of the time, Pallas kernels for 5%

profile of v1, /device:TPU:0, one launch (start us, length us, event | category | flops | bytes accessed | tf_op | source)
XLA Modules:
  0.0 296.5 jit_solution(5602212439445406796)
XLA Ops:
  7.2 1.7 convert_bitcast_fusion.1.shard_ref
  8.9 53.1 %gather_all.1 = bf16[2,2,2,2,2,920,128]{6,5,4,3,2,1,0:T(8,128)(2,1)} custom-call(bf16[920,128]{1,0:T(8,128)(2,1)} %convert_bitcast_fusion.1.shard_ref), custom_call_target="tpu_custom_call" | custom-call | tf_op jit(solution)/shard_map/gather_all/pallas_call | solution.py:396
  62.8 5.8 %slice.161 = bf16[20112,128]{1,0:T(8,128)(2,1)} slice(bf16[29440,128]{1,0:T(8,128)(2,1)} %bitcast.141), slice={[0:20112], [0:128]} | slice | bytes 10297344 | tf_op jit(solution)/shard_map/slice | solution.py:422
  69.3 10.4 %reshape.213 = bf16[768,3352]{1,0:T(8,128)(2,1)} reshape(bf16[20112,128]{1,0:T(8,128)(2,1)} %slice.161) | data formatting | bytes 10297344 | tf_op jit(solution)/shard_map/reshape | solution.py:424
  79.8 4.2 %convolution_convert_fusion.1 = bf16[256,3352]{1,0:T(8,128)(2,1)S(1)} fusion(bf16[768,3352]{1,0:T(8,128)(2,1)} %reshape.213, bf16[1,256,768]{2,1,0:T(8,128)(2,1)S(1)} %copy-done.24, f32[768]{0:T(1024)S(1)} %fusion.112, f32[256]{0:T(256)S(1)} %get-tuple-element.57), kind=kOutput, calls=%fused_computation.4 | convolution fusion | flops 1319704576 | bytes 7262208 | tf_op jit(solution)/shard_map/dot_general | solution.py:439
  84.0 2.3 collective-permute-start
  90.4 2.4 multiply_convert_fusion
  94.3 1.7 slice.182
  96.1 3.2 %reshape.215 = bf16[1536,768]{1,0:T(8,128)(2,1)} reshape(bf16[9216,128]{1,0:T(8,128)(2,1)S(1)} %slice.182) | data formatting | bytes 4718592 | tf_op jit(solution)/shard_map/reshape | solution.py:425
  99.9 0.9 fusion.128
  101.6 0.9 convolution_reduce_fusion
  103.2 2.0 fusion.65
  105.2 0.9 slice.171.x_ref
  106.8 6.5 %inside_forward.1 = f32[256,1536]{1,0:T(8,128)} custom-call(bf16[256,1536]{1,0:T(8,128)(2,1)} %slice.171.x_ref, bf16[256,128]{1,0:T(8,128)(2,1)} %get-tuple-element.49.b_ref, bf16[256,128]{1,0:T(8,128)(2,1)} %get-tuple-element.48.c_ref, f32[256,128]{1,0:T(8,128)} %pad.25.cum_ref, f32[24,256]{1,0:T(8,128)} %bitcast.151, f32[24,256]{1,0:T(8,128)} %copy.46.dt_t_ref), custom_call_target="tpu_custom_call" | custom-call | flops 402653184 | bytes 1572864 | tf_op jit(solution)/shard_map/inside_forward/pallas_call | solution.py:150
  113.3 13.4 %all-gather.5.cloned.1.call-done = bf16[12416,128]{1,0:T(8,128)(2,1)} async-done(((bf16[1552,128]{1,0:T(8,128)(2,1)}), bf16[12416,128]{1,0:T(8,128)(2,1)}) %all-gather.5.cloned.1.call-update) | async-done | bytes 3178512 | tf_op jit(solution)/shard_map/all_gather | solution.py:477
  127.8 4.0 %multiply_reduce_fusion = f32[1536,128]{1,0:T(8,128)S(1)} fusion(bf16[8,1552,128]{2,1,0:T(8,128)(2,1)} %bitcast.150, f32[8,1536]{1,0:T(8,128)S(1)} %fusion.66), kind=kLoop, calls=%fused_computation.3 | loop fusion | flops 4521984 | bytes 3981312 | tf_op jit(solution)/shard_map/reduce_sum | solution.py:488
  131.9 2.7 multiply_reduce_fusion.7
  134.7 1.5 multiply_reduce_fusion.5
  136.2 1.0 copy-done.31
  137.2 2.4 fusion.11
  139.6 1.4 multiply_convert_fusion.1
  141.0 1.2 convolution_convert_fusion.3
  142.2 9.2 %inside_backward.1 = (f32[256,1536]{1,0:T(8,128)}, f32[256,128]{1,0:T(8,128)}, f32[256,128]{1,0:T(8,128)}, f32[256,128]{1,0:T(8,128)}, f32[24,256]{1,0:T(8,128)}) custom-call(bf16[256,1536]{1,0:T(8,128)(2,1)} %slice.171.x_ref, bf16[256,1536]{1,0:T(8,128)(2,1)} %get-tuple-element.47.dy_ref, bf16[256,128]{1,0:T(8,128)(2,1)} %get-tuple-element.49.b_ref, ...), custom_call_target="tpu_custom_call" | custom-call | flops 805306368 | bytes 3145728 | tf_op jit(solution)/shard_map/inside_backward/pallas_call | solution.py:166
  151.4 1.5 copy.52
  152.9 3.3 %convolution_convert_fusion.2 = bf16[1536,768]{1,0:T(8,128)(2,1)} fusion(bf16[1,256,768]{2,1,0:T(8,128)(2,1)} %param.6, f32[256,1536]{1,0:T(8,128)S(1)} %get-tuple-element.37, f32[1536]{0:T(1024)S(1)} %fusion.104, f32[256]{0:T(256)S(1)} %get-tuple-element.59), kind=kOutput, calls=%fused_computation.5 | convolution fusion | flops 606339072 | bytes 4332544 | tf_op jit(solution)/shard_map/dot_general | solution.py:70
  156.2 4.2 %reshape.217.refs_1_ = bf16[9216,128]{1,0:T(8,128)(2,1)S(1)} reshape(bf16[1536,768]{1,0:T(8,128)(2,1)} %convolution_convert_fusion.2) | data formatting | bytes 4718592 | tf_op jit(solution)/shard_map/reshape | solution.py:569
  161.2 0.8 fusion.64
  162.0 2.0 convolution_add_fusion.2
  164.1 3.4 %fusion.14 = f32[1,256,768]{2,1,0:T(8,128)} fusion(bf16[1536,768]{1,0:T(8,128)(2,1)} %reshape.215, bf16[1,256,768]{2,1,0:T(8,128)(2,1)S(1)} %copy-done.25, f32[256,1536]{1,0:T(8,128)S(1)} %copy-done.10, f32[1536]{0:T(1024)S(1)} %fusion.104, f32[256]{0:T(256)S(1)} %copy-done.51), kind=kOutput, calls=%fused_computation.48 | convolution fusion | flops 605552640 | bytes 5118976 | tf_op jit(solution)/shard_map/dot_general | solution.py:498
  167.5 7.2 %all-gather.7.cloned.1.call-done = bf16[12288,128]{1,0:T(8,128)(2,1)} async-done(((bf16[1536,128]{1,0:T(8,128)(2,1)}), bf16[12288,128]{1,0:T(8,128)(2,1)}) %all-gather.7.cloned.1.call-update) | async-done | bytes 3145744 | tf_op jit(solution)/shard_map/all_gather | solution.py:512
  174.7 4.0 %fusion = f32[1536,128]{1,0:T(8,128)S(1)} fusion(bf16[8,1536,128]{2,1,0:T(8,128)(2,1)} %bitcast.148, f32[8,1536]{1,0:T(8,128)} %fusion.64), kind=kLoop, calls=%fused_computation.2 | loop fusion | flops 4521984 | bytes 3981312 | tf_op jit(solution)/shard_map/reduce_sum | solution.py:516
  179.5 1.0 copy-done.8
  181.4 1.0 copy-done.2
  183.0 2.4 multiply_reduce_fusion.4
  188.9 1.5 pad_add_fusion
  190.5 1.9 multiply_reduce_fusion.10
  192.5 1.3 collective-permute-start.1
  194.0 1.8 fusion.19
  195.9 1.2 fusion.134
  197.3 1.1 slice.270
  198.6 1.1 fusion.99
  200.2 5.1 %fusion.40 = (bf16[768]{0:T(1024)(128)(2,1)S(1)}, f32[256]{0:T(256)S(1)}, f32[256,768]{1,0:T(8,128)}) fusion(bf16[1,256,768]{2,1,0:T(8,128)(2,1)S(1)} %copy-done.26, f32[256]{0:T(256)S(1)} %copy-done.65, f32[768]{0:T(1024)S(1)} %copy-done.57, bf16[768,3352]{1,0:T(8,128)(2,1)} %reshape.213, bf16[256,24]{1,0:T(8,128)(2,1)S(1)} %get-tuple-element.34, ...), kind=kOutput, calls=%fused_computation.84 | convolution fusion | flops 1326300160 | bytes 8051200 | tf_op jit(solution)/shard_map/dot_general | solution.py:557
  205.3 4.0 %convolution_convert_fusion = bf16[768,3352]{1,0:T(8,128)(2,1)} fusion(bf16[1,256,768]{2,1,0:T(8,128)(2,1)S(1)} %copy-done.26, f32[768]{0:T(1024)S(1)} %copy-done.57, f32[256]{0:T(256)S(1)} %copy-done.65, bf16[256,24]{1,0:T(8,128)(2,1)S(1)} %get-tuple-element.34, bf16[3,1792]{1,0:T(4,128)(2,1)S(1)} %fusion.99, bf16[253,1792]{1,0:T(8,128)(2,1)S(1)} %copy-done.32, ...), kind=kOutput, calls=%fused_computation | convolution fusion | flops 1328285696 | bytes 7262208 | tf_op jit(solution)/shard_map/dot_general | solution.py:70
  209.3 10.3 %reshape.216.refs_0_ = bf16[20112,128]{1,0:T(8,128)(2,1)} reshape(bf16[768,3352]{1,0:T(8,128)(2,1)} %convolution_convert_fusion) | data formatting | bytes 10297344 | tf_op jit(solution)/shard_map/reshape | solution.py:569
  219.6 2.3 fusion.35
  222.1 2.5 copy-done
  224.6 63.7 %scatter_sum.1 = bf16[920,128]{1,0:T(8,128)(2,1)S(1)} custom-call(bf16[20112,128]{1,0:T(8,128)(2,1)S(1)} %copy-done, bf16[9216,128]{1,0:T(8,128)(2,1)S(1)} %reshape.217.refs_1_, bf16[112,128]{1,0:T(8,128)(2,1)S(1)} %concatenate.35.refs_2_), custom_call_target="tpu_custom_call" | custom-call | tf_op jit(solution)/shard_map/scatter_sum/pallas_call | solution.py:338
  288.3 1.3 multiply_subtract_fusion.1
  (203 shorter events, 18.5 us)
Async XLA Ops:
  7.2 119.5 %all-gather.5.cloned.1.call-start = ((), (), s32[]{:S(2)}) async-start(), calls=%async_computation | async-start | bytes 3575808 | tf_op jit(solution)/shard_map/all_gather | solution.py:477
  62.8 17.0 %copy-start.56 = (f32[768]{0:T(1024)}, f32[768]{0:T(1024)S(1)}, u32[]{:S(2)}) copy-start(f32[768]{0:T(1024)S(1)} %fusion.112) | copy-start | bytes 9220
  62.8 5.8 %copy-start.24 = (bf16[1,256,768]{2,1,0:T(8,128)(2,1)S(1)}, bf16[1,256,768]{2,1,0:T(8,128)(2,1)}, u32[]{:S(2)}) copy-start(bf16[1,256,768]{2,1,0:T(8,128)(2,1)} %param.5) | copy-start | bytes 1179652
  69.3 10.5 %copy-start.64 = (f32[256]{0:T(256)}, f32[256]{0:T(256)S(1)}, u32[]{:S(2)}) copy-start(f32[256]{0:T(256)S(1)} %get-tuple-element.57) | copy-start | bytes 3076
  83.9 6.2 %copy-start.27 = (bf16[256,3352]{1,0:T(8,128)(2,1)}, bf16[256,3352]{1,0:T(8,128)(2,1)S(1)}, u32[]{:S(2)}) copy-start(bf16[256,3352]{1,0:T(8,128)(2,1)S(1)} %convolution_convert_fusion.1) | copy-start | bytes 5148676
  84.0 6.2 %collective-permute-start = (bf16[3,1792]{1,0:T(4,128)(2,1)S(1)}, bf16[3,1792]{1,0:T(4,128)(2,1)S(1)}, u32[]{:S(2)}, u32[]{:S(2)}) collective-permute-start(bf16[3,1792]{1,0:T(4,128)(2,1)S(1)} %slice.162), channel_id=1, source_target_pairs={{0,4},{4,8},{8,12},{12,16},{16,20},{20,24},{24,28},{1,5},{5,9},{9,... | collective-permute-start | bytes 32264 | tf_op jit(solution)/shard_map/ppermute | solution.py:37
  86.3 74.9 %copy-start.52 = (pred[1536]{0:T(1024)(128)(4,1)}, pred[1536]{0:T(1024)(128)(4,1)S(1)}, u32[]{:S(2)}) copy-start(pred[1536]{0:T(1024)(128)(4,1)S(1)} %fusion.103) | copy-start | bytes 4612
  86.3 74.9 %copy-start.37 = (s32[1536]{0:T(1024)}, s32[1536]{0:T(1024)S(1)}, u32[]{:S(2)}) copy-start(s32[1536]{0:T(1024)S(1)} %get-tuple-element.70) | copy-start | bytes 18436
  88.8 14.3 %copy-start.41 = (f32[256,24]{0,1:T(8,128)}, f32[256,24]{0,1:T(8,128)S(1)}, u32[]{:S(2)}) copy-start(f32[256,24]{0,1:T(8,128)S(1)} %fusion.58) | copy-start | bytes 73732
  89.9 2.9 copy-start.11
  90.3 2.5 copy-start.1
  94.1 80.6 %all-gather.7.cloned.1.call-start = ((), (), s32[]{:S(2)}) async-start(), calls=%async_computation.1 | async-start | bytes 3538944 | tf_op jit(solution)/shard_map/all_gather | solution.py:512
  96.0 3.9 %copy-start.61 = (f32[24]{0:T(128)S(1)}, f32[24]{0:T(128)}, u32[]{:S(2)}) copy-start(f32[24]{0:T(128)} %copy-done.60) | copy-start | bytes 292
  102.4 33.8 %copy-start.54 = (f32[1536]{0:T(1024)}, f32[1536]{0:T(1024)S(1)}, u32[]{:S(2)}) copy-start(f32[1536]{0:T(1024)S(1)} %convolution_reduce_fusion) | copy-start | bytes 18436
  127.8 4.0 %copy-start.20 = (f32[256,1536]{1,0:T(8,128)S(1)}, f32[256,1536]{1,0:T(8,128)}, u32[]{:S(2)}) copy-start(f32[256,1536]{1,0:T(8,128)} %fusion.65) | copy-start | bytes 4718596
  127.8 4.0 %copy-start.28 = (bf16[256,3352]{1,0:T(8,128)(2,1)S(1)}, bf16[256,3352]{1,0:T(8,128)(2,1)}, u32[]{:S(2)}) copy-start(bf16[256,3352]{1,0:T(8,128)(2,1)} %copy-done.27) | copy-start | bytes 5148676
  131.8 2.8 copy-start.16
  131.8 2.8 copy-start.13
  131.9 2.8 copy-start.22
  134.6 18.3 %copy-start.9 = (f32[256,1536]{1,0:T(8,128)}, f32[256,1536]{1,0:T(8,128)S(1)}, u32[]{:S(2)}) copy-start(f32[256,1536]{1,0:T(8,128)S(1)} %get-tuple-element.37) | copy-start | bytes 4718596
  134.6 18.3 %copy-start.50 = (f32[256]{0:T(256)}, f32[256]{0:T(256)S(1)}, u32[]{:S(2)}) copy-start(f32[256]{0:T(256)S(1)} %get-tuple-element.59) | copy-start | bytes 3076
  134.7 2.5 copy-start.31
  141.0 10.4 %copy-start.15 = (bf16[256,1536]{1,0:T(8,128)(2,1)}, bf16[256,1536]{1,0:T(8,128)(2,1)S(1)}, u32[]{:S(2)}) copy-start(bf16[256,1536]{1,0:T(8,128)(2,1)S(1)} %get-tuple-element.46) | copy-start | bytes 2359300
  160.5 3.6 %copy-start.10 = (f32[256,1536]{1,0:T(8,128)S(1)}, f32[256,1536]{1,0:T(8,128)}, u32[]{:S(2)}) copy-start(f32[256,1536]{1,0:T(8,128)} %copy-done.9) | copy-start | bytes 4718596
  160.5 3.6 %copy-start.25 = (bf16[1,256,768]{2,1,0:T(8,128)(2,1)S(1)}, bf16[1,256,768]{2,1,0:T(8,128)(2,1)}, u32[]{:S(2)}) copy-start(bf16[1,256,768]{2,1,0:T(8,128)(2,1)} %param.5) | copy-start | bytes 1179652
  160.5 3.6 %copy-start.51 = (f32[256]{0:T(256)S(1)}, f32[256]{0:T(256)}, u32[]{:S(2)}) copy-start(f32[256]{0:T(256)} %copy-done.50) | copy-start | bytes 3076
  174.7 4.0 %copy-start.17 = (f32[1536,128]{1,0:T(8,128)S(1)}, f32[1536,128]{1,0:T(8,128)}, u32[]{:S(2)}) copy-start(f32[1536,128]{1,0:T(8,128)} %copy-done.16) | copy-start | bytes 2359300
  174.7 4.3 %copy-start.12 = (f32[256,1536]{1,0:T(8,128)S(1)}, f32[256,1536]{1,0:T(8,128)}, u32[]{:S(2)}) copy-start(f32[256,1536]{1,0:T(8,128)} %copy-done.11) | copy-start | bytes 4718596
  174.7 4.3 %copy-start.40 = (f32[256,128]{1,0:T(8,128)S(1)}, f32[256,128]{1,0:T(8,128)}, u32[]{:S(2)}) copy-start(f32[256,128]{1,0:T(8,128)} %get-tuple-element.12) | copy-start | bytes 393220
  183.0 2.5 copy-start.43
  183.0 2.5 copy-start.45
  183.0 2.5 copy-start.47
  183.0 2.5 copy-start.49
  186.0 2.4 copy-start.5
  186.1 2.9 copy-start.6
  190.5 3.5 %copy-start.19 = (f32[256,1536]{1,0:T(8,128)S(1)}, f32[256,1536]{1,0:T(8,128)}, u32[]{:S(2)}) copy-start(f32[256,1536]{1,0:T(8,128)} %copy-done.18) | copy-start | bytes 4718596
  190.5 3.5 %copy-start.34 = (f32[24,256]{0,1:T(8,128)S(1)}, f32[24,256]{0,1:T(8,128)}, u32[]{:S(2)}) copy-start(f32[24,256]{0,1:T(8,128)} %copy.52) | copy-start | bytes 73732
  190.5 3.5 %copy-start.39 = (f32[256,128]{1,0:T(8,128)S(1)}, f32[256,128]{1,0:T(8,128)}, u32[]{:S(2)}) copy-start(f32[256,128]{1,0:T(8,128)} %get-tuple-element.15) | copy-start | bytes 393220
  192.5 6.1 %collective-permute-start.1 = (f32[3,1792]{1,0:T(4,128)}, f32[3,1792]{1,0:T(4,128)}, u32[]{:S(2)}, u32[]{:S(2)}) collective-permute-start(f32[3,1792]{1,0:T(4,128)} %pad_add_fusion.1), channel_id=1, source_target_pairs={{4,0},{8,4},{12,8},{16,12},{20,16},{24,20},{28,24},{5,1},{9,5},{13... | collective-permute-start | bytes 64520 | tf_op jit(solution)/shard_map/ppermute | solution.py:37
  194.0 3.2 %copy-start.67 = (f32[1,128]{1,0:T(1,128)S(1)}, f32[1,128]{1,0:T(1,128)}, u32[]{:S(2)}) copy-start(f32[1,128]{1,0:T(1,128)} %copy-done.66) | copy-start | bytes 1540
  194.0 3.3 %copy-start.21 = (bf16[259,1792]{1,0:T(8,128)(2,1)S(1)}, bf16[259,1792]{1,0:T(8,128)(2,1)}, u32[]{:S(2)}) copy-start(bf16[259,1792]{1,0:T(8,128)(2,1)} %pad_add_fusion) | copy-start | bytes 2784772
  195.9 2.6 copy-start.70
  209.3 10.3 %copy-start.23 = (bf16[1,256,768]{2,1,0:T(8,128)(2,1)S(1)}, bf16[1,256,768]{2,1,0:T(8,128)(2,1)}, u32[]{:S(2)}) copy-start(bf16[1,256,768]{2,1,0:T(8,128)(2,1)} %param.6) | copy-start | bytes 1179652
  209.3 10.3 %copy-start.63 = (f32[256]{0:T(256)S(1)}, f32[256]{0:T(256)}, u32[]{:S(2)}) copy-start(f32[256]{0:T(256)} %get-tuple-element.56) | copy-start | bytes 3076
  222.1 2.5 copy-start
  224.6 63.7 %copy-start.29 = (f32[117760]{0:T(1024)S(1)}, f32[117760]{0:T(1024)}, u32[]{:S(2)}) copy-start(f32[117760]{0:T(1024)} %param.7) | copy-start | bytes 1413124
  224.6 63.7 %copy-start.35 = (f32[117760]{0:T(1024)S(1)}, f32[117760]{0:T(1024)}, u32[]{:S(2)}) copy-start(f32[117760]{0:T(1024)} %param.8) | copy-start | bytes 1413124
  224.6 63.7 %copy-start.36 = (f32[117760]{0:T(1024)S(1)}, f32[117760]{0:T(1024)}, u32[]{:S(2)}) copy-start(f32[117760]{0:T(1024)} %param.9) | copy-start | bytes 1413124
  (29 other events, 44.7 us)
Sparse Core Ops, SparseCore 0:
  94.2 32.4 all-gather.4
  142.3 32.3 all-gather.6
